TPU v7x, 256 devices: a whole 4x4x8 slice. The times are simulated.
256 devices in a mesh: section: 4 (over x), seq: 16 (over z, y_lo), dp: 4 (over y_hi, core).
Axes of the slice: x: 4, y: 4 (y_hi: 2, y_lo: 2; y = y_hi * 2 + y_lo), z: 8, core: 2. Of those that a mesh axis runs over, the one named last changes fastest.
Arguments:
- main_hidden: bfloat16 [4, 4, 2048, 7168], P('section', 'dp', 'seq'), may hold values from -6 to 6
- embedded: bfloat16 [4, 4, 2048, 7168], P('section', 'dp', 'seq'), may hold values from -6 to 6
- cotangent: bfloat16 [4, 4, 2048, 7168], P('section', 'dp', 'seq'), may hold values from -6 to 6
- slot_token: int32 [4, 4, 2, 96], P('section', 'dp', None, 'seq'), may hold values from 0 to 127, as said below
- slot_count: int32 [4, 4, 2, 16], P('section', 'dp', None, 'seq'), may hold values from 1 to 6, as said below
- route_gate: float32 [4, 4, 2, 96], P('section', 'dp', None, 'seq'), may hold values from 0.2 to 2
- norm_gain: float32 [2, 2, 7168], replicated, may hold values from 0.5 to 1.5
- expert_weight: bfloat16 [2, 3, 7168, 2048], P(None, None, 'seq', 'dp'), may hold values from -0.0625 to 0.0625
Outputs:
- hidden_grad: bfloat16 [4, 4, 2048, 7168], P('section', 'dp', 'seq')
- expert_grad: bfloat16 [4, 2, 3, 7168, 2048], P('section', None, None, 'seq', 'dp')
- gain_grad: float32 [4, 2, 2, 7168], P('section', None, None, ('seq', 'dp'))
Inputs may be any that keep to these rules, and one draw needn't show every extreme that they name: `slot_token`: the slots of one device and depth name distinct positions of that device's block. `slot_count`: in every micro-batch, sequence and depth some device has all 6 slots live.
All inputs are finite; a program needn't handle non-finite values.
Results may differ from a plain program's by a relative error of at most 0.0077.
Values may be sent and summed in bfloat16 or wider, within the bound.
A program may use at most 128 MiB of HBM per device.

v0:
```python
import jax
import jax.numpy as jnp
from jax import lax
from jax.sharding import PartitionSpec as P

eps_norm = 1e-06


def from_behind(value, axis, steps):
    count = lax.axis_size(axis)
    pairs = [(source, (source + steps) % count) for source in range(count)]
    return lax.ppermute(value, axis, pairs)


def from_behind_2(array, axis, by):
    size = lax.axis_size(axis)
    pairs = [(i, i + by) for i in range(size) if 0 <= i + by < size]
    return lax.ppermute(array, axis, pairs)


def normed(value):
    wide = value.astype(jnp.float32)
    scale = lax.rsqrt(jnp.mean(wide * wide, axis=-1, keepdims=True) + eps_norm)
    return (wide * scale, scale)


def norm_back(grad, unit, scale):
    inner = jnp.mean(grad * unit, axis=-1, keepdims=True)
    return (grad - unit * inner) * scale


def contract_rows(left, right):
    return lax.dot_general(
        left, right, (((0,), (0,)), ((), ())), preferred_element_type=jnp.float32
    )


def contract_last(left, right):
    return lax.dot_general(
        left, right, (((1,), (1,)), ((), ())), preferred_element_type=jnp.float32
    )


def spread_rows(rows):
    parts = lax.all_to_all(rows, "seq", split_axis=1, concat_axis=0, tiled=True)
    return lax.all_gather(parts, "dp", axis=0, tiled=True)


def return_rows(partial_rows, capacity):
    blocks = partial_rows.reshape(
        lax.axis_size("dp"), lax.axis_size("seq"), capacity, partial_rows.shape[1]
    )
    back = lax.all_to_all(blocks, "seq", split_axis=1, concat_axis=3, tiled=True)
    total = lax.psum_scatter(back, "dp", scatter_dimension=0, tiled=True)
    return total.reshape(capacity, -1)


def pre_grads(d_act, gate_in, up_in):
    sig = jax.nn.sigmoid(gate_in)
    d_gate = (d_act * up_in * sig * (1.0 + gate_in * (1.0 - sig))).astype(jnp.bfloat16)
    d_up = (d_act * jax.nn.silu(gate_in)).astype(jnp.bfloat16)
    return (d_gate, d_up)


def local(
    main_hidden, embedded, cotangent, slot_token, slot_count, route_gate, norm_gain, expert_weight
):
    depths = norm_gain.shape[0]
    tokens_here = main_hidden.shape[2]
    capacity = slot_token.shape[3]
    hidden = from_behind(main_hidden, "section", 1)[0, 0]
    own_rows = embedded[0, 0]
    ahead = from_behind_2(own_rows[:depths], "seq", -1)
    padded = jnp.concatenate([own_rows, ahead], 0)
    places = jnp.arange(capacity, dtype=jnp.int32)
    current = hidden
    saved = []
    for depth in range(depths):
        shifted = padded[depth + 1 : depth + 1 + tokens_here]
        unit_h, scale_h = normed(current)
        unit_e, scale_e = normed(shifted)
        mixed = (unit_h * norm_gain[depth, 0] + unit_e * norm_gain[depth, 1]).astype(jnp.bfloat16)
        tokens = slot_token[0, 0, depth]
        live = places < slot_count[0, 0, depth, 0]
        weight = route_gate[0, 0, depth] * live.astype(jnp.float32)
        rows = mixed[tokens] * live[:, None].astype(jnp.bfloat16)
        quarter = spread_rows(rows)
        gate_part = jnp.dot(quarter, expert_weight[depth, 0], preferred_element_type=jnp.float32)
        up_part = jnp.dot(quarter, expert_weight[depth, 1], preferred_element_type=jnp.float32)
        gate_in, up_in = lax.psum((gate_part, up_part), "seq")
        act = (jax.nn.silu(gate_in) * up_in).astype(jnp.bfloat16)
        result = return_rows(contract_last(act, expert_weight[depth, 2]), capacity)
        current = (
            mixed.astype(jnp.float32).at[tokens].add(result * weight[:, None]).astype(jnp.bfloat16)
        )
        saved.append((unit_h, scale_h, unit_e, tokens, live, weight, quarter, gate_in, up_in, act))
    grad = cotangent[0, 0].astype(jnp.float32)
    weight_grads = [None] * depths
    gain_terms = [None] * depths
    for depth in reversed(range(depths)):
        unit_h, scale_h, unit_e, tokens, live, weight, quarter, gate_in, up_in, act = saved[depth]
        dout = (grad[tokens] * weight[:, None]).astype(jnp.bfloat16)
        dout_quarter = spread_rows(dout)
        act_part = jnp.dot(
            dout_quarter, expert_weight[depth, 2], preferred_element_type=jnp.float32
        )
        down_grad = contract_rows(dout_quarter, act)
        d_act = lax.psum(act_part, "seq")
        d_gate, d_up = pre_grads(d_act, gate_in, up_in)
        gate_grad = contract_rows(quarter, d_gate)
        up_grad = contract_rows(quarter, d_up)
        partial_rows = contract_last(d_gate, expert_weight[depth, 0]) + contract_last(
            d_up, expert_weight[depth, 1]
        )
        d_rows = return_rows(partial_rows, capacity)
        d_mixed = grad.at[tokens].add(d_rows * live[:, None].astype(jnp.float32))
        gain_terms[depth] = jnp.stack([jnp.sum(d_mixed * unit_h, 0), jnp.sum(d_mixed * unit_e, 0)])
        weight_grads[depth] = jnp.stack([gate_grad, up_grad, down_grad])
        grad = norm_back(d_mixed * norm_gain[depth, 0], unit_h, scale_h)
    gain_grad = lax.psum_scatter(
        jnp.stack(gain_terms), ("seq", "dp"), scatter_dimension=2, tiled=True
    )
    hidden_grad = from_behind(grad.astype(jnp.bfloat16)[None, None], "section", -1)
    expert_grad = jnp.stack(weight_grads).astype(jnp.bfloat16)[None]
    return (hidden_grad, expert_grad, gain_grad[None])


def solution(mesh):
    return jax.shard_map(
        local,
        mesh=mesh,
        in_specs=(
            P("section", "dp", "seq", None),
            P("section", "dp", "seq", None),
            P("section", "dp", "seq", None),
            P("section", "dp", None, "seq"),
            P("section", "dp", None, "seq"),
            P("section", "dp", None, "seq"),
            P(),
            P(None, None, "seq", "dp"),
        ),
        out_specs=(
            P("section", "dp", "seq", None),
            P("section", None, None, "seq", "dp"),
            P("section", None, None, ("seq", "dp")),
        ),
        check_vma=False,
    )
```

profile of v0, /device:TPU:2, one launch (start us, length us, event | category | flops | bytes accessed | tf_op | source)
XLA Modules:
  0.0 1106.0 jit_solution(5909491801143368804)
XLA Ops:
  18.5 33.0 %collective-permute-done = bf16[1,1,128,7168]{3,2,1,0:T(8,128)(2,1)S(1)} collective-permute-done((bf16[1,1,128,7168]{3,2,1,0:T(8,128)(2,1)}, bf16[1,1,128,7168]{3,2,1,0:T(8,128)(2,1)S(1)}, u32[]{:S(2)}, u32[]{:S(2)}) %collective-permute-start) | collective-permute-done | bytes 1835040 | tf_op jit(solution)/shard_map/ppermute | solution.py:12
  58.1 19.9 %all_to_all.118 = bf16[6,16,448]{2,0,1:T(8,128)(2,1)S(1)} all-to-all(bf16[6,16,448]{2,0,1:T(8,128)(2,1)S(1)} %copy.77), channel_id=1, replica_groups=mesh['section'=4,'seq'=16,'dp'=4] {'seq'}, dimensions={1} | all-to-all | bytes 172032 | tf_op jit(solution)/shard_map/all_to_all | solution.py:45
  78.1 8.0 all_gather.13
  90.7 138.8 %all-reduce.10.cloned.1.call-done = (f32[384,512]{1,0:T(8,128)}, f32[384,512]{1,0:T(8,128)}) async-done(((f32[384,512]{1,0:T(8,128)}, f32[384,512]{1,0:T(8,128)}), (f32[384,512]{1,0:T(8,128)}, f32[384,512]{1,0:T(8,128)})) %all-reduce.10.cloned.1.call-update) | async-done | bytes 1572880 | tf_op jit(solution)/shard_map/psum | solution.py:90
  233.2 21.8 %all_to_all.119 = f32[4,16,6,448]{3,0,2,1:T(4,128)S(1)} all-to-all(f32[4,16,6,448]{3,0,2,1:T(4,128)S(1)} %copy.79), channel_id=1, replica_groups=mesh['section'=4,'seq'=16,'dp'=4] {'seq'}, dimensions={1} | all-to-all | bytes 1376256 | tf_op jit(solution)/shard_map/all_to_all | solution.py:53
  269.6 9.1 all-to-all-done
  278.7 10.3 all_gather.12
  291.7 5.1 scatter_custom_fusion
  314.1 7.1 all-to-all-done.3
  321.2 7.6 all_gather.14
  333.5 145.2 %all-reduce.8.cloned.1.call-done = (f32[384,512]{1,0:T(8,128)}, f32[384,512]{1,0:T(8,128)}, f32[384,512]{1,0:T(8,128)}) async-done(((f32[384,512]{1,0:T(8,128)}, f32[384,512]{1,0:T(8,128)}, f32[384,512]{1,0:T(8,128)}), (f32[384,512]{1,0:T(8,128)}, f32[384,512]{1,0:T(8,128)}, f32[384,512]{1,0:T(8,128)})) %all-reduce.8.cloned.1.call-update) | async-done | bytes 2359312 | tf_op jit(solution)/shard_map/psum | solution.py:90
  490.9 21.0 %all_to_all.120 = f32[4,16,6,448]{3,0,2,1:T(4,128)S(1)} all-to-all(f32[4,16,6,448]{3,0,2,1:T(4,128)S(1)} %copy.84), channel_id=1, replica_groups=mesh['section'=4,'seq'=16,'dp'=4] {'seq'}, dimensions={1} | all-to-all | bytes 1376256 | tf_op jit(solution)/shard_map/all_to_all | solution.py:53
  516.5 31.8 %reduce-scatter.9.cloned.1.call-done = f32[1,1,6,7168]{3,2,1,0:T(8,128)} async-done(((f32[4,1,6,7168]{3,2,1,0:T(8,128)}), f32[1,1,6,7168]{3,2,1,0:T(8,128)}) %reduce-scatter.9.cloned.1.call-update) | async-done | bytes 172048 | tf_op jit(solution)/shard_map/reduce_scatter | solution.py:54
  548.3 5.1 scatter_custom_fusion.1
  564.0 16.6 %all_to_all.121 = bf16[6,16,448]{2,0,1:T(8,128)(2,1)S(1)} all-to-all(bf16[6,16,448]{2,0,1:T(8,128)(2,1)S(1)} %copy.87), channel_id=1, replica_groups=mesh['section'=4,'seq'=16,'dp'=4] {'seq'}, dimensions={1} | all-to-all | bytes 172032 | tf_op jit(solution)/shard_map/all_to_all | solution.py:45
  580.7 7.6 all_gather.15
  591.3 134.4 %all-reduce.6.cloned.1.call-done = f32[384,512]{1,0:T(8,128)} async-done(((f32[384,512]{1,0:T(8,128)}), f32[384,512]{1,0:T(8,128)}) %all-reduce.6.cloned.1.call-update) | async-done | bytes 786448 | tf_op jit(solution)/shard_map/psum | solution.py:108
  738.8 5.8 all-to-all-start.6
  751.5 9.0 all-to-all-done.6
  771.2 27.7 %reduce-scatter.11.cloned.1.call-done = f32[1,1,6,7168]{3,2,1,0:T(8,128)} async-done(((f32[4,1,6,7168]{3,2,1,0:T(8,128)}), f32[1,1,6,7168]{3,2,1,0:T(8,128)}) %reduce-scatter.11.cloned.1.call-update) | async-done | bytes 172048 | tf_op jit(solution)/shard_map/reduce_scatter | solution.py:54
  798.9 5.1 scatter_custom_fusion.2
  811.2 6.8 copy.96
  818.0 7.9 reshape.298
  829.3 265.3 %reduce-scatter.13.cloned.1.call-done = f32[112,4]{1,0:T(8,128)} async-done(((f32[7168,4]{1,0:T(8,128)}), f32[112,4]{1,0:T(8,128)}) %reduce-scatter.13.cloned.1.call-update) | async-done | bytes 1808
  (165 shorter events, 141.3 us)
Async XLA Ops:
  7.2 222.3 %all-reduce.10.cloned.1.call-start = ((), (), s32[]{:S(2)}) async-start(), calls=%async_computation.17 | async-start | bytes 3145728 | tf_op jit(solution)/shard_map/psum | solution.py:90
  8.1 6.6 collective-permute-start.1
  9.4 42.0 %collective-permute-start = (bf16[1,1,128,7168]{3,2,1,0:T(8,128)(2,1)}, bf16[1,1,128,7168]{3,2,1,0:T(8,128)(2,1)S(1)}, u32[]{:S(2)}, u32[]{:S(2)}) collective-permute-start(bf16[1,1,128,7168]{3,2,1,0:T(8,128)(2,1)} %param.8), channel_id=1, source_target_pairs={{0,64},{64,128},{128,192},{192,0},{1,65},{65,129},{129,193},{193,1... | collective-permute-start | bytes 5505032 | tf_op jit(solution)/shard_map/ppermute | solution.py:12
  11.8 279.9 %copy-start.25 = (s32[6]{0:T(128)}, s32[6]{0:T(128)S(1)}, u32[]{:S(2)}) copy-start(s32[6]{0:T(128)S(1)} %get-tuple-element.32) | copy-start | bytes 76
  13.1 42.3 %copy-start.18 = (s32[1024]{0:T(1024)}, s32[1024]{0:T(1024)S(1)}, u32[]{:S(2)}) copy-start(s32[1024]{0:T(1024)S(1)} %pad_clamp_fusion) | copy-start | bytes 12292
  18.4 36.9 %copy-start.5 = (bf16[128,7168]{1,0:T(8,128)(2,1)}, bf16[128,7168]{1,0:T(8,128)(2,1)S(1)}, u32[]{:S(2)}) copy-start(bf16[128,7168]{1,0:T(8,128)(2,1)S(1)} %get-tuple-element.19) | copy-start | bytes 5505028
  18.4 36.9 %copy-start.23 = (f32[128]{0:T(128)}, f32[128]{0:T(128)S(1)}, u32[]{:S(2)}) copy-start(f32[128]{0:T(128)S(1)} %add_rsqrt_fusion.2) | copy-start | bytes 1540
  90.7 201.0 %reduce-scatter.7.cloned.1.call-start = ((), (), s32[]{:S(2)}) async-start(), calls=%async_computation.11 | async-start | bytes 1146880 | tf_op jit(solution)/shard_map/reduce_scatter | solution.py:54
  231.1 25.6 %copy-start.7 = (bf16[384,512]{1,0:T(8,128)(2,1)}, bf16[384,512]{1,0:T(8,128)(2,1)S(1)}, u32[]{:S(2)}) copy-start(bf16[384,512]{1,0:T(8,128)(2,1)S(1)} %multiply_convert_fusion.5) | copy-start | bytes 1179652
  264.6 34.9 %copy-start.21 = (f32[6]{0:T(128)}, f32[6]{0:T(128)S(1)}, u32[]{:S(2)}) copy-start(f32[6]{0:T(128)S(1)} %get-tuple-element.30) | copy-start | bytes 76
  265.4 13.2 %all-to-all-start = ((bf16[6,16,448]{2,0,1:T(8,128)(2,1)}), bf16[6,16,448]{2,0,1:T(8,128)(2,1)S(1)}, u32[]{:S(2)}, u32[]{:S(2)}) async-start(bf16[6,16,448]{2,0,1:T(8,128)(2,1)} %copy.76), calls=%async_computation | async-start | bytes 262144 | tf_op jit(solution)/shard_map/all_to_all | solution.py:45
  289.0 22.8 %copy-start.16 = (bf16[384,448]{1,0:T(8,128)(2,1)}, bf16[384,448]{1,0:T(8,128)(2,1)S(1)}, u32[]{:S(2)}) copy-start(bf16[384,448]{1,0:T(8,128)(2,1)S(1)} %all_gather.12) | copy-start | bytes 1032196
  306.5 14.7 %all-to-all-start.3 = ((bf16[6,16,448]{2,0,1:T(8,128)(2,1)}), bf16[6,16,448]{2,0,1:T(8,128)(2,1)S(1)}, u32[]{:S(2)}, u32[]{:S(2)}) async-start(bf16[6,16,448]{2,0,1:T(8,128)(2,1)} %copy.82), calls=%async_computation.4 | async-start | bytes 262144 | tf_op jit(solution)/shard_map/all_to_all | solution.py:45
  311.6 167.1 %all-reduce.8.cloned.1.call-start = ((), (), s32[]{:S(2)}) async-start(), calls=%async_computation.16 | async-start | bytes 4718592 | tf_op jit(solution)/shard_map/psum | solution.py:90
  333.4 214.8 %reduce-scatter.9.cloned.1.call-start = ((), (), s32[]{:S(2)}) async-start(), calls=%async_computation.12 | async-start | bytes 1146880 | tf_op jit(solution)/shard_map/reduce_scatter | solution.py:54
  515.8 210.0 %all-reduce.6.cloned.1.call-start = ((), (), s32[]{:S(2)}) async-start(), calls=%async_computation.13 | async-start | bytes 1572864 | tf_op jit(solution)/shard_map/psum | solution.py:108
  738.8 21.6 %all-to-all-start.6 = ((f32[4,16,6,448]{3,0,2,1:T(4,128)}), f32[4,16,6,448]{3,0,2,1:T(4,128)}, u32[]{:S(2)}, u32[]{:S(2)}) async-start(f32[4,16,6,448]{3,0,2,1:T(4,128)} %copy.89), calls=%async_computation.8 | async-start | bytes 1572864 | tf_op jit(solution)/shard_map/all_to_all | solution.py:53
  744.6 54.4 %reduce-scatter.11.cloned.1.call-start = ((), (), s32[]{:S(2)}) async-start(), calls=%async_computation.14 | async-start | bytes 1146880 | tf_op jit(solution)/shard_map/reduce_scatter | solution.py:54
  751.5 16.8 %copy-start.8 = (bf16[384,512]{1,0:T(8,128)(2,1)S(1)}, bf16[384,512]{1,0:T(8,128)(2,1)}, u32[]{:S(2)}) copy-start(bf16[384,512]{1,0:T(8,128)(2,1)} %copy-done.7) | copy-start | bytes 1179652
  751.5 16.8 %copy-start.11 = (bf16[384,448]{1,0:T(8,128)(2,1)S(1)}, bf16[384,448]{1,0:T(8,128)(2,1)}, u32[]{:S(2)}) copy-start(bf16[384,448]{1,0:T(8,128)(2,1)} %copy-done.10) | copy-start | bytes 1032196
  765.4 329.3 %reduce-scatter.13.cloned.1.call-start = ((), (), s32[]{:S(2)}) async-start(), calls=%async_computation.15 | async-start | bytes 3727360
  768.3 35.7 %copy-start.20 = (f32[128]{0:T(128)S(1)}, f32[128]{0:T(128)}, u32[]{:S(2)}) copy-start(f32[128]{0:T(128)} %copy-done.19) | copy-start | bytes 1540
  768.3 35.7 %copy-start.24 = (f32[128]{0:T(128)S(1)}, f32[128]{0:T(128)}, u32[]{:S(2)}) copy-start(f32[128]{0:T(128)} %copy-done.23) | copy-start | bytes 1540
  810.5 285.8 %collective-permute-start.2 = (bf16[1,1,128,7168]{3,2,1,0:T(8,128)(2,1)}, bf16[1,1,128,7168]{3,2,1,0:T(8,128)(2,1)}, u32[]{:S(2)}, u32[]{:S(2)}) collective-permute-start(bf16[1,1,128,7168]{3,2,1,0:T(8,128)(2,1)} %fusion.32), channel_id=1, source_target_pairs={{0,192},{64,0},{128,64},{192,128},{1,193},{65,1},{129,65},{193,129... | collective-permute-start | bytes 5505032 | tf_op jit(solution)/shard_map/ppermute | solution.py:12
  (16 other events, 63.3 us)
Sparse Core Ops, SparseCore 0:
  90.8 138.6 all-reduce.9
  256.9 34.7 reduce-scatter.6
  333.6 145.0 all-reduce.7
  515.9 32.3 reduce-scatter.8
  591.5 134.2 all-reduce.5
  765.5 33.4 reduce-scatter.10
  826.1 268.5 reduce-scatter.12
where the time goes:
time: 1110 us
  waiting for transfers between devices  804 us (72%)
  blocking collectives  113 us (10%)
  local copies, waits for them, and re-layouts  63.1 us (6%)
  other arithmetic  60.9 us (5%)
  matrix products  31.8 us (3%)
  starting transfers between devices  18.4 us (2%)
  between operations  14.6 us (1%)
    psum x2, waiting for transfers between devices, local(): gate_in, up_in = lax.psum((gate_part, up_part), 'seq')  284 us
    unnamed x8, waiting for transfers between devices  265 us
    psum x1, waiting for transfers between devices, local(): d_act = lax.psum(act_part, 'seq')  134 us
    reduce_scatter x3, waiting for transfers between devices, return_rows(): total = lax.psum_scatter(back, 'dp', scatter_dimension=0, tiled=True)  62.3 us
    all_to_all x2, blocking collectives, return_rows(): lax.all_to_all(blocks, 'seq', split_axis=1, concat_axis=3, tiled=True)  42.8 us
    all_to_all x2, blocking collectives, spread_rows(): parts = lax.all_to_all(rows, 'seq', split_axis=1, concat_axis=0, tiled=True)  36.5 us
    all_gather x4, blocking collectives, spread_rows(): return lax.all_gather(parts, 'dp', axis=0, tiled=True)  33.6 us
    ppermute x2, waiting for transfers between devices, from_behind(): return lax.ppermute(value, axis, pairs)  33 us
  transfers between devices with their start and end apart: 13, of which 11 were waited for; matrix products, arithmetic and copies ran while one was open for 5% of the time, Pallas kernels for 0%

commit v1 on v0

--- a/solution.py
+++ b/solution.py
@@ -105,7 +105,7 @@
             dout_quarter, expert_weight[depth, 2], preferred_element_type=jnp.float32
         )
         down_grad = contract_rows(dout_quarter, act)
-        d_act = lax.psum(act_part, "seq")
+        d_act = jnp.sum(lax.all_gather(act_part, "seq"), axis=0)
         d_gate, d_up = pre_grads(d_act, gate_in, up_in)
         gate_grad = contract_rows(quarter, d_gate)
         up_grad = contract_rows(quarter, d_up)

time: 1110 us -> 1490 us (1.34)
  waiting for transfers between devices: 804 us -> 1140 us
  blocking collectives: 113 us -> 146 us
    all_gather x0 -> x2, waiting for transfers between devices: none -> 486 us  [local(): d_act = jnp.sum(lax.all_gather(act_part, 'seq'), axis=0)]
    psum x1 -> x0, waiting for transfers between devices: 134 us -> none  [local(): d_act = lax.psum(act_part, 'seq')]
    all_to_all x2 -> x4, blocking collectives: 36.5 us -> 64.8 us  [spread_rows(): parts = lax.all_to_all(rows, 'seq', split_axis=1, concat_axis=0, tiled=True)]
    all_to_all x2 -> x0, waiting for transfers between devices: 16.2 us -> none  [spread_rows(): parts = lax.all_to_all(rows, 'seq', split_axis=1, concat_axis=0, tiled=True)]
    unnamed x8 -> x9, waiting for transfers between devices: 265 us -> 266 us
  transfers between devices with their start and end apart: 13 -> 12, of which waited for: 11 -> 10; matrix products, arithmetic and copies ran while one was open for 5% -> 5% of each run, Pallas kernels for 0% -> 0%
where the time goes in v1:
time: 1490 us; the launch traced here: 1480 us
  waiting for transfers between devices  1140 us (77%)
  blocking collectives  146 us (10%)
  other arithmetic  74.7 us (5%)
  local copies, waits for them, and re-layouts  62.8 us (4%)
  matrix products  30.9 us (2%)
    all_gather x2, waiting for transfers between devices, local(): d_act = jnp.sum(lax.all_gather(act_part, 'seq'), axis=0)  486 us
    psum x2, waiting for transfers between devices, local(): gate_in, up_in = lax.psum((gate_part, up_part), 'seq')  281 us
    unnamed x9, waiting for transfers between devices  266 us
    all_to_all x4, blocking collectives, spread_rows(): parts = lax.all_to_all(rows, 'seq', split_axis=1, concat_axis=0, tiled=True)  64.8 us
    reduce_scatter x3, waiting for transfers between devices, return_rows(): total = lax.psum_scatter(back, 'dp', scatter_dimension=0, tiled=True)  59.7 us
    all_to_all x2, blocking collectives, return_rows(): lax.all_to_all(blocks, 'seq', split_axis=1, concat_axis=3, tiled=True)  43.6 us
    all_gather x4, blocking collectives, spread_rows(): return lax.all_gather(parts, 'dp', axis=0, tiled=True)  37.4 us
    ppermute x2, waiting for transfers between devices, from_behind(): return lax.ppermute(value, axis, pairs)  33.1 us
  transfers between devices with their start and end apart: 12, of which 10 were waited for; matrix products, arithmetic and copies ran while one was open for 5% of the time, Pallas kernels for 0%

profile of v1, /device:TPU:2, one launch (start us, length us, event | category | flops | bytes accessed | tf_op | source)
XLA Modules:
  0.0 1483.3 jit_solution(1301371497363858820)
XLA Ops:
  18.4 33.1 %collective-permute-done = bf16[1,1,128,7168]{3,2,1,0:T(8,128)(2,1)S(1)} collective-permute-done((bf16[1,1,128,7168]{3,2,1,0:T(8,128)(2,1)}, bf16[1,1,128,7168]{3,2,1,0:T(8,128)(2,1)S(1)}, u32[]{:S(2)}, u32[]{:S(2)}) %collective-permute-start) | collective-permute-done | bytes 1835040 | tf_op jit(solution)/shard_map/ppermute | solution.py:12
  58.1 19.9 %all_to_all.118 = bf16[6,16,448]{2,0,1:T(8,128)(2,1)S(1)} all-to-all(bf16[6,16,448]{2,0,1:T(8,128)(2,1)S(1)} %copy.77), channel_id=1, replica_groups=mesh['section'=4,'seq'=16,'dp'=4] {'seq'}, dimensions={1} | all-to-all | bytes 172032 | tf_op jit(solution)/shard_map/all_to_all | solution.py:45
  78.1 8.0 all_gather.27
  90.7 138.8 %all-reduce.7.cloned.1.call-done = (f32[384,512]{1,0:T(8,128)}, f32[384,512]{1,0:T(8,128)}) async-done(((f32[384,512]{1,0:T(8,128)}, f32[384,512]{1,0:T(8,128)}), (f32[384,512]{1,0:T(8,128)}, f32[384,512]{1,0:T(8,128)})) %all-reduce.7.cloned.1.call-update) | async-done | bytes 1572880 | tf_op jit(solution)/shard_map/psum | solution.py:90
  233.2 21.8 %all_to_all.119 = f32[4,16,6,448]{3,0,2,1:T(4,128)S(1)} all-to-all(f32[4,16,6,448]{3,0,2,1:T(4,128)S(1)} %copy.79), channel_id=1, replica_groups=mesh['section'=4,'seq'=16,'dp'=4] {'seq'}, dimensions={1} | all-to-all | bytes 1376256 | tf_op jit(solution)/shard_map/all_to_all | solution.py:53
  264.7 12.3 all_to_all.120
  277.1 9.1 all_gather.24
  304.5 16.0 %all_to_all.121 = bf16[6,16,448]{2,0,1:T(8,128)(2,1)S(1)} all-to-all(bf16[6,16,448]{2,0,1:T(8,128)(2,1)S(1)} %copy.82), channel_id=1, replica_groups=mesh['section'=4,'seq'=16,'dp'=4] {'seq'}, dimensions={1} | all-to-all | bytes 172032 | tf_op jit(solution)/shard_map/all_to_all | solution.py:45
  320.5 12.3 all_gather.28
  337.5 223.5 %all-gather.5.cloned.1.call-done = f32[6144,512]{1,0:T(8,128)} async-done(((f32[384,512]{1,0:T(8,128)}), f32[6144,512]{1,0:T(8,128)}) %all-gather.5.cloned.1.call-update) | async-done | bytes 12582928 | tf_op jit(solution)/shard_map/all_gather | solution.py:108
  561.0 7.0 reduce_sum.108
  568.1 142.5 %all-reduce.5.cloned.1.call-done = (f32[384,512]{1,0:T(8,128)}, f32[384,512]{1,0:T(8,128)}) async-done(((f32[384,512]{1,0:T(8,128)}, f32[384,512]{1,0:T(8,128)}), (f32[384,512]{1,0:T(8,128)}, f32[384,512]{1,0:T(8,128)})) %all-reduce.5.cloned.1.call-update) | async-done | bytes 1572880 | tf_op jit(solution)/shard_map/psum | solution.py:90
  722.9 21.8 %all_to_all.122 = f32[4,16,6,448]{3,0,2,1:T(4,128)S(1)} all-to-all(f32[4,16,6,448]{3,0,2,1:T(4,128)S(1)} %copy.84), channel_id=1, replica_groups=mesh['section'=4,'seq'=16,'dp'=4] {'seq'}, dimensions={1} | all-to-all | bytes 1376256 | tf_op jit(solution)/shard_map/all_to_all | solution.py:53
  749.2 32.1 %reduce-scatter.9.cloned.1.call-done = f32[1,1,6,7168]{3,2,1,0:T(8,128)} async-done(((f32[4,1,6,7168]{3,2,1,0:T(8,128)}), f32[1,1,6,7168]{3,2,1,0:T(8,128)}) %reduce-scatter.9.cloned.1.call-update) | async-done | bytes 172048 | tf_op jit(solution)/shard_map/reduce_scatter | solution.py:54
  797.1 16.6 %all_to_all.123 = bf16[6,16,448]{2,0,1:T(8,128)(2,1)S(1)} all-to-all(bf16[6,16,448]{2,0,1:T(8,128)(2,1)S(1)} %copy.87), channel_id=1, replica_groups=mesh['section'=4,'seq'=16,'dp'=4] {'seq'}, dimensions={1} | all-to-all | bytes 172032 | tf_op jit(solution)/shard_map/all_to_all | solution.py:45
  813.7 7.9 all_gather.29
  824.6 262.2 %all-gather.7.cloned.1.call-done = f32[6144,512]{1,0:T(8,128)} async-done(((f32[384,512]{1,0:T(8,128)}), f32[6144,512]{1,0:T(8,128)}) %all-gather.7.cloned.1.call-update) | async-done | bytes 12582928 | tf_op jit(solution)/shard_map/all_gather | solution.py:108
  1086.9 7.0 reduce_sum.114
  1107.0 8.4 all-to-all-start.6
  1121.3 17.0 %all-to-all-done.6 = f32[4,16,6,448]{3,0,2,1:T(4,128)} async-done(((f32[4,16,6,448]{3,0,2,1:T(4,128)}), f32[4,16,6,448]{3,0,2,1:T(4,128)}, u32[]{:S(2)}, u32[]{:S(2)}) %all-to-all-start.6) | async-done | bytes 688160 | tf_op jit(solution)/shard_map/all_to_all | solution.py:53
  1148.8 27.3 %reduce-scatter.11.cloned.1.call-done = f32[1,1,6,7168]{3,2,1,0:T(8,128)} async-done(((f32[4,1,6,7168]{3,2,1,0:T(8,128)}), f32[1,1,6,7168]{3,2,1,0:T(8,128)}) %reduce-scatter.11.cloned.1.call-update) | async-done | bytes 172048 | tf_op jit(solution)/shard_map/reduce_scatter | solution.py:54
  1188.3 6.9 copy.96
  1195.2 7.9 reshape.300
  1206.5 265.5 %reduce-scatter.13.cloned.1.call-done = f32[112,4]{1,0:T(8,128)} async-done(((f32[7168,4]{1,0:T(8,128)}), f32[112,4]{1,0:T(8,128)}) %reduce-scatter.13.cloned.1.call-update) | async-done | bytes 1808
  (170 shorter events, 143.7 us)
Async XLA Ops:
  7.2 222.3 %all-reduce.7.cloned.1.call-start = ((), (), s32[]{:S(2)}) async-start(), calls=%async_computation.18 | async-start | bytes 3145728 | tf_op jit(solution)/shard_map/psum | solution.py:90
  8.1 6.5 collective-permute-start.1
  9.4 42.0 %collective-permute-start = (bf16[1,1,128,7168]{3,2,1,0:T(8,128)(2,1)}, bf16[1,1,128,7168]{3,2,1,0:T(8,128)(2,1)S(1)}, u32[]{:S(2)}, u32[]{:S(2)}) collective-permute-start(bf16[1,1,128,7168]{3,2,1,0:T(8,128)(2,1)} %param.8), channel_id=1, source_target_pairs={{0,64},{64,128},{128,192},{192,0},{1,65},{65,129},{129,193},{193,1... | collective-permute-start | bytes 5505032 | tf_op jit(solution)/shard_map/ppermute | solution.py:12
  11.8 278.5 %copy-start.26 = (s32[6]{0:T(128)}, s32[6]{0:T(128)S(1)}, u32[]{:S(2)}) copy-start(s32[6]{0:T(128)S(1)} %get-tuple-element.31) | copy-start | bytes 76
  13.1 42.3 %copy-start.19 = (s32[1024]{0:T(1024)}, s32[1024]{0:T(1024)S(1)}, u32[]{:S(2)}) copy-start(s32[1024]{0:T(1024)S(1)} %pad_clamp_fusion) | copy-start | bytes 12292
  18.3 37.0 %copy-start.5 = (bf16[128,7168]{1,0:T(8,128)(2,1)}, bf16[128,7168]{1,0:T(8,128)(2,1)S(1)}, u32[]{:S(2)}) copy-start(bf16[128,7168]{1,0:T(8,128)(2,1)S(1)} %get-tuple-element.18) | copy-start | bytes 5505028
  18.4 37.0 %copy-start.24 = (f32[128]{0:T(128)}, f32[128]{0:T(128)S(1)}, u32[]{:S(2)}) copy-start(f32[128]{0:T(128)S(1)} %add_rsqrt_fusion.2) | copy-start | bytes 1540
  90.7 199.6 %reduce-scatter.7.cloned.1.call-start = ((), (), s32[]{:S(2)}) async-start(), calls=%async_computation.11 | async-start | bytes 1146880 | tf_op jit(solution)/shard_map/reduce_scatter | solution.py:54
  231.1 25.6 %copy-start.7 = (bf16[384,512]{1,0:T(8,128)(2,1)}, bf16[384,512]{1,0:T(8,128)(2,1)S(1)}, u32[]{:S(2)}) copy-start(bf16[384,512]{1,0:T(8,128)(2,1)S(1)} %multiply_convert_fusion.5) | copy-start | bytes 1179652
  256.7 6.6 copy-start.27
  256.8 304.3 %all-gather.5.cloned.1.call-start = ((), (), s32[]{:S(2)}) async-start(), calls=%async_computation.14 | async-start | bytes 13369344 | tf_op jit(solution)/shard_map/all_gather | solution.py:108
  264.5 30.7 %copy-start.22 = (f32[6]{0:T(128)}, f32[6]{0:T(128)S(1)}, u32[]{:S(2)}) copy-start(f32[6]{0:T(128)S(1)} %get-tuple-element.29) | copy-start | bytes 76
  289.3 421.3 %all-reduce.5.cloned.1.call-start = ((), (), s32[]{:S(2)}) async-start(), calls=%async_computation.17 | async-start | bytes 3145728 | tf_op jit(solution)/shard_map/psum | solution.py:90
  337.5 443.9 %reduce-scatter.9.cloned.1.call-start = ((), (), s32[]{:S(2)}) async-start(), calls=%async_computation.12 | async-start | bytes 1146880 | tf_op jit(solution)/shard_map/reduce_scatter | solution.py:54
  748.5 338.3 %all-gather.7.cloned.1.call-start = ((), (), s32[]{:S(2)}) async-start(), calls=%async_computation.15 | async-start | bytes 13369344 | tf_op jit(solution)/shard_map/all_gather | solution.py:108
  1107.0 31.3 %all-to-all-start.6 = ((f32[4,16,6,448]{3,0,2,1:T(4,128)}), f32[4,16,6,448]{3,0,2,1:T(4,128)}, u32[]{:S(2)}, u32[]{:S(2)}) async-start(f32[4,16,6,448]{3,0,2,1:T(4,128)} %copy.89), calls=%async_computation.8 | async-start | bytes 1572864 | tf_op jit(solution)/shard_map/all_to_all | solution.py:53
  1115.4 60.7 %reduce-scatter.11.cloned.1.call-start = ((), (), s32[]{:S(2)}) async-start(), calls=%async_computation.13 | async-start | bytes 1146880 | tf_op jit(solution)/shard_map/reduce_scatter | solution.py:54
  1121.3 24.6 %copy-start.18 = (f32[7168]{0:T(1024)S(1)}, f32[7168]{0:T(1024)}, u32[]{:S(2)}) copy-start(f32[7168]{0:T(1024)} %get-tuple-element.8) | copy-start | bytes 86020
  1121.3 24.7 %copy-start.8 = (bf16[384,512]{1,0:T(8,128)(2,1)S(1)}, bf16[384,512]{1,0:T(8,128)(2,1)}, u32[]{:S(2)}) copy-start(bf16[384,512]{1,0:T(8,128)(2,1)} %copy-done.7) | copy-start | bytes 1179652
  1121.3 24.7 %copy-start.12 = (bf16[384,448]{1,0:T(8,128)(2,1)S(1)}, bf16[384,448]{1,0:T(8,128)(2,1)}, u32[]{:S(2)}) copy-start(bf16[384,448]{1,0:T(8,128)(2,1)} %copy-done.11) | copy-start | bytes 1032196
  1143.2 328.8 %reduce-scatter.13.cloned.1.call-start = ((), (), s32[]{:S(2)}) async-start(), calls=%async_computation.16 | async-start | bytes 3727360
  1146.0 35.2 %copy-start.21 = (f32[128]{0:T(128)S(1)}, f32[128]{0:T(128)}, u32[]{:S(2)}) copy-start(f32[128]{0:T(128)} %copy-done.20) | copy-start | bytes 1540
  1146.0 35.2 %copy-start.25 = (f32[128]{0:T(128)S(1)}, f32[128]{0:T(128)}, u32[]{:S(2)}) copy-start(f32[128]{0:T(128)} %copy-done.24) | copy-start | bytes 1540
  1187.7 286.0 %collective-permute-start.2 = (bf16[1,1,128,7168]{3,2,1,0:T(8,128)(2,1)}, bf16[1,1,128,7168]{3,2,1,0:T(8,128)(2,1)}, u32[]{:S(2)}, u32[]{:S(2)}) collective-permute-start(bf16[1,1,128,7168]{3,2,1,0:T(8,128)(2,1)} %fusion.32), channel_id=1, source_target_pairs={{0,192},{64,0},{128,64},{192,128},{1,193},{65,1},{129,65},{193,129... | collective-permute-start | bytes 5505032 | tf_op jit(solution)/shard_map/ppermute | solution.py:12
  (16 other events, 44.2 us)
Sparse Core Ops, SparseCore 0:
  90.8 138.6 all-reduce.6
  256.9 33.3 reduce-scatter.6
  292.0 268.9 all-gather.4
  563.6 146.9 all-reduce.4
  748.6 32.6 reduce-scatter.8
  824.8 262.0 all-gather.6
  1143.4 32.6 reduce-scatter.10
  1203.3 268.6 reduce-scatter.12
